TPU v7x, 256 devices: a whole 4x4x8 slice. The times are simulated.
256 devices in a mesh: blk: 64 (over x, y_lo, z), heads: 4 (over y_hi, core).
Axes of the slice: x: 4, y: 4 (y_hi: 2, y_lo: 2; y = y_hi * 2 + y_lo), z: 8, core: 2. Of those that a mesh axis runs over, the one named last changes fastest.
Arguments:
- queries: float32 [4096, 8192], P('blk', 'heads'), may hold values from -6 to 6
- visual_keys: float32 [65536, 1024], P('blk', 'heads'), may hold values from -6 to 6
- projected_values: float32 [65536, 1024], P('blk', 'heads'), may hold values from -6 to 6
- valid_lengths: int32 [64], P('blk'), may hold values from 256 to 1024, as said below
Outputs:
- attended: float32 [4096, 8192], P('blk', 'heads')
Inputs may be any that keep to these rules, and one draw needn't show every extreme that they name: `valid_lengths`: some block has all 1024 tokens valid in every draw.
All inputs are finite; a program needn't handle non-finite values.
Results may differ from a plain program's by a relative error of at most 0.0003.
Values sent between devices are 32-bit elements; how exact they have to be, the bound alone decides.
No kernel may reach another device: no remote copies, remote signals or barrier semaphores. Data moves between devices by JAX's collectives and lax.ppermute only.
A program may use at most 64 MiB of HBM per device.

v0:
```python
import jax
import jax.numpy as jnp
from jax import lax
from jax.sharding import PartitionSpec as P

HEAD_DIM = 128
SPAN = 6


def passed_along(shard, axis, by):
    size = lax.axis_size(axis)
    return lax.ppermute(shard, axis, [(i, (i + by) % size) for i in range(size)])


def attend(partial_value, query_tile, key_tile, value_tile, usable):
    peak_score, weight_sum, numerator = partial_value
    scores = jnp.einsum("qhgd,khd->hgqk", query_tile, key_tile, precision=lax.Precision.HIGHEST)
    scores = jnp.where(usable, scores, -1e30)
    new_peak = jnp.maximum(peak_score, jnp.max(scores, axis=-1))
    weights = jnp.where(usable, jnp.exp(scores - new_peak[..., None]), 0.0)
    factor = jnp.exp(peak_score - new_peak)
    weight_sum = weight_sum * factor + jnp.sum(weights, axis=-1)
    numerator = numerator * jnp.transpose(factor, (2, 0, 1))[..., None] + jnp.einsum(
        "hgqk,khd->qhgd", weights, value_tile, precision=lax.Precision.HIGHEST
    )
    return (new_peak, weight_sum, numerator)


def per_device(queries, visual_keys, projected_values, valid_lengths):
    shard_blocks = lax.axis_size("blk")
    window = min(SPAN, shard_blocks // 2)
    left_reach = window // 2 - 1
    right_reach = window // 2
    device_pos = lax.axis_index("blk")
    query_rows = queries.shape[0]
    key_rows = visual_keys.shape[0]
    kv_heads = visual_keys.shape[1] // HEAD_DIM
    group_size = queries.shape[1] // (HEAD_DIM * kv_heads)
    query_tile = (queries * HEAD_DIM ** (-0.5)).reshape(query_rows, kv_heads, group_size, HEAD_DIM)
    key_tile = visual_keys.reshape(key_rows, kv_heads, HEAD_DIM)
    value_tile = projected_values.reshape(key_rows, kv_heads, HEAD_DIM)
    positions = jnp.arange(key_rows, dtype=jnp.int32)
    own_usable = positions < valid_lengths[0]
    initial = (
        jnp.full((kv_heads, group_size, query_rows), -1e30, jnp.float32),
        jnp.zeros((kv_heads, group_size, query_rows), jnp.float32),
        jnp.zeros((query_rows, kv_heads, group_size, HEAD_DIM), jnp.float32),
    )

    def query_usable(offset):
        owner_block = device_pos - offset
        return own_usable & (owner_block >= 0) & (owner_block < shard_blocks)

    moving = passed_along(query_tile, "blk", -left_reach)
    partial_value = attend(initial, moving, key_tile, value_tile, query_usable(-left_reach))

    def advance(position, carried):
        arrived = passed_along((carried[0], carried[1], carried[2], carried[3]), "blk", 1)
        outcome = attend(
            (arrived[1], arrived[2], arrived[3]),
            arrived[0],
            key_tile,
            value_tile,
            query_usable(position - left_reach),
        )
        return (arrived[0],) + outcome

    carried = lax.fori_loop(1, window, advance, (moving,) + partial_value)
    final_state = passed_along((carried[1], carried[2], carried[3]), "blk", -right_reach)
    weight_sum = final_state[1]
    numerator = final_state[2]
    normed = numerator / jnp.transpose(weight_sum, (2, 0, 1))[..., None]
    return normed.reshape(query_rows, kv_heads * group_size * HEAD_DIM)


def solution(mesh):
    return jax.shard_map(
        per_device,
        mesh=mesh,
        in_specs=(P("blk", "heads"), P("blk", "heads"), P("blk", "heads"), P("blk")),
        out_specs=P("blk", "heads"),
        check_vma=False,
    )
```

profile of v0, /device:TPU:16, one launch (start us, length us, event | category | flops | bytes accessed | tf_op | source)
XLA Modules:
  0.0 252.2 jit_solution(15848718381238051673)
XLA Ops:
  0.0 1.2 multiply_bitcast_fusion
  2.1 9.2 %collective-permute-start.4 = (f32[64,2,8,128]{3,2,0,1:T(8,128)}, f32[64,2,8,128]{3,2,0,1:T(8,128)}, u32[]{:S(2)}, u32[]{:S(2)}) collective-permute-start(f32[64,2,8,128]{3,2,0,1:T(8,128)} %copy.20), channel_id=1, source_target_pairs={{0,248},{4,252},{8,0},{12,4},{16,8},{20,12},{24,16},{28,20},{32,24... | collective-permute-start | bytes 1572872 | tf_op jit(solution)/shard_map/ppermute | solution.py:12
  12.0 1.6 copy.21
  14.2 1.3 copy.30
  15.6 18.5 %collective-permute-done.4 = f32[64,2,8,128]{3,2,0,1:T(8,128)} collective-permute-done((f32[64,2,8,128]{3,2,0,1:T(8,128)}, f32[64,2,8,128]{3,2,0,1:T(8,128)}, u32[]{:S(2)}, u32[]{:S(2)}) %collective-permute-start.4) | collective-permute-done | bytes 524320 | tf_op jit(solution)/shard_map/ppermute | solution.py:12
  34.1 6.2 %bitcast_reduce_fusion.1 = (f32[2,8,64]{1,2,0:T(8,128)S(1)}, f32[2,64,8,1024]{3,2,1,0:T(8,128)}) fusion(pred[1024]{0:T(1024)(128)(4,1)S(1)} %fusion.46, f32[64,2,8,128]{3,2,0,1:T(8,128)} %collective-permute-done.4, f32[1024,2,128,1]{0,2,3,1:T(8,128)S(1)} %bitcast.97), kind=kOutput, calls=%fused_computation.26 | convolution fusion | flops 1612708864 | bytes 5772288 | tf_op jit(solution)/shard_map/qhgd,khd->hgqk/dot_general | solution.py:17
  40.4 3.2 %fusion.31 = f32[2,8,64]{1,2,0:T(8,128)S(1)} fusion(f32[2,64,8,1024]{3,2,1,0:T(8,128)} %get-tuple-element.367, f32[2,8,64]{1,2,0:T(8,128)S(1)} %broadcast_maximum_fusion, pred[1024]{0:T(1024)(128)(4,1)S(1)} %fusion.46), kind=kLoop, calls=%fused_computation.30 | loop fusion | flops 4193280 | bytes 4203520 | tf_op jit(solution)/shard_map/reduce_sum | solution.py:22
  43.7 5.8 %fusion.40 = f32[64,2,8,128]{3,2,0,1:T(8,128)S(1)} fusion(f32[1024,2,128,1]{0,2,3,1:T(8,128)S(1)} %bitcast.99, f32[2,64,8,1024]{3,2,1,0:T(8,128)} %get-tuple-element.367, f32[2,8,64]{1,2,0:T(8,128)S(1)} %broadcast_maximum_fusion, pred[1024]{0:T(1024)(128)(4,1)S(1)} %fusion.46, f32[64,2,8]{2,0,1:T(8,128)S(1)} %get-tuple-element.364), kind=kOutput, calls=%fused_computation.37 | convolution fusion | flops 1613889536 | bytes 5776384 | tf_op jit(solution)/shard_map/hgqk,khd->qhgd/dot_general | solution.py:23
  49.6 1.9 copy.25
  51.6 166.1 %while.24 = (s32[]{:T(128)}, f32[64,2,8,128]{3,0,2,1:T(8,128)}, f32[2,8,64]{2,1,0:T(8,128)S(1)}, f32[2,8,64]{2,1,0:T(8,128)S(1)}, f32[64,2,8,128]{3,0,2,1:T(8,12...) while((s32[]{:T(128)}, f32[64,2,8,128]{3,0,2,1:T(8,128)}, ...), condition=%wide.region_5.6_spmd.clone, body=%wide.region_2.5_spmd.clone.sunk | while | flops 3230930944 | bytes 21590356 | solution.py:68
  51.7 2.9 %collective-permute-start.3 = (f32[64,2,8,128]{3,0,2,1:T(8,128)S(1)}, f32[64,2,8,128]{3,0,2,1:T(8,128)}, u32[]{:S(2)}, u32[]{:S(2)}) collective-permute-start(f32[64,2,8,128]{3,0,2,1:T(8,128)S(1)} %get-tuple-element.448), channel_id=1, source_target_pairs={{0,4},{4,8},{8,12},{12,16},{16,20},{20,24},{24,28},{28,32},{32,36}... | collective-permute-start | bytes 1572872 | tf_op jit(solution)/shard_map/while/body/eval_jaxpr/ppermute | solution.py:12
  55.3 15.5 %collective-permute-done = f32[64,2,8,128]{3,0,2,1:T(8,128)S(1)} collective-permute-done((f32[64,2,8,128]{3,0,2,1:T(8,128)}, f32[64,2,8,128]{3,0,2,1:T(8,128)S(1)}, u32[]{:S(2)}, u32[]{:S(2)}) %collective-permute-start) | collective-permute-done | bytes 524320 | tf_op jit(solution)/shard_map/while/body/eval_jaxpr/ppermute | solution.py:12
  70.8 3.7 %bitcast_reduce_fusion.3 = (f32[2,8,64]{2,1,0:T(8,128)S(1)}, f32[2,1024,64,8]{1,2,3,0:T(8,128)S(1)}) fusion(pred[1024]{0:T(1024)(128)(4,1)S(1)} %fusion.62, f32[64,2,8,128]{3,0,2,1:T(8,128)S(1)} %collective-permute-done, f32[1024,2,128]{2,0,1:T(8,128)S(1)} %get-tuple-element.463), kind=kOutput, calls=%fused_computation.2.clone.1 | convolution fusion | flops 1612708864 | bytes 5772288 | tf_op jit(solution)/shard_map/while/body/eval_jaxpr/qhgd,khd->hgqk/dot_general | solution.py:17
  76.3 4.7 %collective-permute-done.3 = f32[64,2,8,128]{3,0,2,1:T(8,128)} collective-permute-done((f32[64,2,8,128]{3,0,2,1:T(8,128)S(1)}, f32[64,2,8,128]{3,0,2,1:T(8,128)}, u32[]{:S(2)}, u32[]{:S(2)}) %collective-permute-start.3) | collective-permute-done | bytes 524320 | tf_op jit(solution)/shard_map/while/body/eval_jaxpr/ppermute | solution.py:12
  81.0 5.4 %multiply_add_fusion.5 = f32[64,2,8,128]{3,0,2,1:T(8,128)S(1)} fusion(f32[64,2,8,128]{3,0,2,1:T(8,128)} %collective-permute-done.3, f32[64,2,8]{0,2,1:T(8,128)S(1)} %get-tuple-element.430, f32[1024,2,128]{2,0,1:T(8,128)S(1)} %get-tuple-element.464, f32[2,1024,64,8]{1,2,3,0:T(8,128)S(1)} %get-tuple-element.429, ...), kind=kOutput, calls=%fused_computation.16.clone.1 | convolution fusion | flops 1614020608 | bytes 6300672 | tf_op jit(solution)/shard_map/while/body/eval_jaxpr/hgqk,khd->qhgd/dot_general | solution.py:23
  87.5 18.3 %collective-permute-done = f32[64,2,8,128]{3,0,2,1:T(8,128)S(1)} collective-permute-done((f32[64,2,8,128]{3,0,2,1:T(8,128)}, f32[64,2,8,128]{3,0,2,1:T(8,128)S(1)}, u32[]{:S(2)}, u32[]{:S(2)}) %collective-permute-start) | collective-permute-done | bytes 524320 | tf_op jit(solution)/shard_map/while/body/eval_jaxpr/ppermute | solution.py:12
  105.7 3.7 %bitcast_reduce_fusion.3 = (f32[2,8,64]{2,1,0:T(8,128)S(1)}, f32[2,1024,64,8]{1,2,3,0:T(8,128)S(1)}) fusion(pred[1024]{0:T(1024)(128)(4,1)S(1)} %fusion.62, f32[64,2,8,128]{3,0,2,1:T(8,128)S(1)} %collective-permute-done, f32[1024,2,128]{2,0,1:T(8,128)S(1)} %get-tuple-element.463), kind=kOutput, calls=%fused_computation.2.clone.1 | convolution fusion | flops 1612708864 | bytes 5772288 | tf_op jit(solution)/shard_map/while/body/eval_jaxpr/qhgd,khd->hgqk/dot_general | solution.py:17
  111.2 3.9 %collective-permute-done.3 = f32[64,2,8,128]{3,0,2,1:T(8,128)} collective-permute-done((f32[64,2,8,128]{3,0,2,1:T(8,128)S(1)}, f32[64,2,8,128]{3,0,2,1:T(8,128)}, u32[]{:S(2)}, u32[]{:S(2)}) %collective-permute-start.3) | collective-permute-done | bytes 524320 | tf_op jit(solution)/shard_map/while/body/eval_jaxpr/ppermute | solution.py:12
  115.1 5.4 %multiply_add_fusion.5 = f32[64,2,8,128]{3,0,2,1:T(8,128)S(1)} fusion(f32[64,2,8,128]{3,0,2,1:T(8,128)} %collective-permute-done.3, f32[64,2,8]{0,2,1:T(8,128)S(1)} %get-tuple-element.430, f32[1024,2,128]{2,0,1:T(8,128)S(1)} %get-tuple-element.464, f32[2,1024,64,8]{1,2,3,0:T(8,128)S(1)} %get-tuple-element.429, ...), kind=kOutput, calls=%fused_computation.16.clone.1 | convolution fusion | flops 1614020608 | bytes 6300672 | tf_op jit(solution)/shard_map/while/body/eval_jaxpr/hgqk,khd->qhgd/dot_general | solution.py:23
  121.6 18.3 %collective-permute-done = f32[64,2,8,128]{3,0,2,1:T(8,128)S(1)} collective-permute-done((f32[64,2,8,128]{3,0,2,1:T(8,128)}, f32[64,2,8,128]{3,0,2,1:T(8,128)S(1)}, u32[]{:S(2)}, u32[]{:S(2)}) %collective-permute-start) | collective-permute-done | bytes 524320 | tf_op jit(solution)/shard_map/while/body/eval_jaxpr/ppermute | solution.py:12
  139.8 3.7 %bitcast_reduce_fusion.3 = (f32[2,8,64]{2,1,0:T(8,128)S(1)}, f32[2,1024,64,8]{1,2,3,0:T(8,128)S(1)}) fusion(pred[1024]{0:T(1024)(128)(4,1)S(1)} %fusion.62, f32[64,2,8,128]{3,0,2,1:T(8,128)S(1)} %collective-permute-done, f32[1024,2,128]{2,0,1:T(8,128)S(1)} %get-tuple-element.463), kind=kOutput, calls=%fused_computation.2.clone.1 | convolution fusion | flops 1612708864 | bytes 5772288 | tf_op jit(solution)/shard_map/while/body/eval_jaxpr/qhgd,khd->hgqk/dot_general | solution.py:17
  145.3 3.0 %collective-permute-done.3 = f32[64,2,8,128]{3,0,2,1:T(8,128)} collective-permute-done((f32[64,2,8,128]{3,0,2,1:T(8,128)S(1)}, f32[64,2,8,128]{3,0,2,1:T(8,128)}, u32[]{:S(2)}, u32[]{:S(2)}) %collective-permute-start.3) | collective-permute-done | bytes 524320 | tf_op jit(solution)/shard_map/while/body/eval_jaxpr/ppermute | solution.py:12
  148.3 5.4 %multiply_add_fusion.5 = f32[64,2,8,128]{3,0,2,1:T(8,128)S(1)} fusion(f32[64,2,8,128]{3,0,2,1:T(8,128)} %collective-permute-done.3, f32[64,2,8]{0,2,1:T(8,128)S(1)} %get-tuple-element.430, f32[1024,2,128]{2,0,1:T(8,128)S(1)} %get-tuple-element.464, f32[2,1024,64,8]{1,2,3,0:T(8,128)S(1)} %get-tuple-element.429, ...), kind=kOutput, calls=%fused_computation.16.clone.1 | convolution fusion | flops 1614020608 | bytes 6300672 | tf_op jit(solution)/shard_map/while/body/eval_jaxpr/hgqk,khd->qhgd/dot_general | solution.py:23
  154.8 18.3 %collective-permute-done = f32[64,2,8,128]{3,0,2,1:T(8,128)S(1)} collective-permute-done((f32[64,2,8,128]{3,0,2,1:T(8,128)}, f32[64,2,8,128]{3,0,2,1:T(8,128)S(1)}, u32[]{:S(2)}, u32[]{:S(2)}) %collective-permute-start) | collective-permute-done | bytes 524320 | tf_op jit(solution)/shard_map/while/body/eval_jaxpr/ppermute | solution.py:12
  173.1 3.7 %bitcast_reduce_fusion.3 = (f32[2,8,64]{2,1,0:T(8,128)S(1)}, f32[2,1024,64,8]{1,2,3,0:T(8,128)S(1)}) fusion(pred[1024]{0:T(1024)(128)(4,1)S(1)} %fusion.62, f32[64,2,8,128]{3,0,2,1:T(8,128)S(1)} %collective-permute-done, f32[1024,2,128]{2,0,1:T(8,128)S(1)} %get-tuple-element.463), kind=kOutput, calls=%fused_computation.2.clone.1 | convolution fusion | flops 1612708864 | bytes 5772288 | tf_op jit(solution)/shard_map/while/body/eval_jaxpr/qhgd,khd->hgqk/dot_general | solution.py:17
  178.6 2.1 collective-permute-done.3
  180.7 5.4 %multiply_add_fusion.5 = f32[64,2,8,128]{3,0,2,1:T(8,128)S(1)} fusion(f32[64,2,8,128]{3,0,2,1:T(8,128)} %collective-permute-done.3, f32[64,2,8]{0,2,1:T(8,128)S(1)} %get-tuple-element.430, f32[1024,2,128]{2,0,1:T(8,128)S(1)} %get-tuple-element.464, f32[2,1024,64,8]{1,2,3,0:T(8,128)S(1)} %get-tuple-element.429, ...), kind=kOutput, calls=%fused_computation.16.clone.1 | convolution fusion | flops 1614020608 | bytes 6300672 | tf_op jit(solution)/shard_map/while/body/eval_jaxpr/hgqk,khd->qhgd/dot_general | solution.py:23
  187.2 18.3 %collective-permute-done = f32[64,2,8,128]{3,0,2,1:T(8,128)S(1)} collective-permute-done((f32[64,2,8,128]{3,0,2,1:T(8,128)}, f32[64,2,8,128]{3,0,2,1:T(8,128)S(1)}, u32[]{:S(2)}, u32[]{:S(2)}) %collective-permute-start) | collective-permute-done | bytes 524320 | tf_op jit(solution)/shard_map/while/body/eval_jaxpr/ppermute | solution.py:12
  205.4 3.7 %bitcast_reduce_fusion.3 = (f32[2,8,64]{2,1,0:T(8,128)S(1)}, f32[2,1024,64,8]{1,2,3,0:T(8,128)S(1)}) fusion(pred[1024]{0:T(1024)(128)(4,1)S(1)} %fusion.62, f32[64,2,8,128]{3,0,2,1:T(8,128)S(1)} %collective-permute-done, f32[1024,2,128]{2,0,1:T(8,128)S(1)} %get-tuple-element.463), kind=kOutput, calls=%fused_computation.2.clone.1 | convolution fusion | flops 1612708864 | bytes 5772288 | tf_op jit(solution)/shard_map/while/body/eval_jaxpr/qhgd,khd->hgqk/dot_general | solution.py:17
  210.9 1.3 collective-permute-done.3
  212.2 5.4 %multiply_add_fusion.5 = f32[64,2,8,128]{3,0,2,1:T(8,128)S(1)} fusion(f32[64,2,8,128]{3,0,2,1:T(8,128)} %collective-permute-done.3, f32[64,2,8]{0,2,1:T(8,128)S(1)} %get-tuple-element.430, f32[1024,2,128]{2,0,1:T(8,128)S(1)} %get-tuple-element.464, f32[2,1024,64,8]{1,2,3,0:T(8,128)S(1)} %get-tuple-element.429, ...), kind=kOutput, calls=%fused_computation.16.clone.1 | convolution fusion | flops 1614020608 | bytes 6300672 | tf_op jit(solution)/shard_map/while/body/eval_jaxpr/hgqk,khd->qhgd/dot_general | solution.py:23
  217.8 32.8 %collective-permute-done.6 = f32[2,8,64]{2,1,0:T(8,128)S(1)} collective-permute-done((f32[2,8,64]{2,1,0:T(8,128)S(1)}, f32[2,8,64]{2,1,0:T(8,128)S(1)}, u32[]{:S(2)}, u32[]{:S(2)}) %collective-permute-start.6) | collective-permute-done | bytes 4128 | tf_op jit(solution)/shard_map/ppermute | solution.py:12
  (74 shorter events, 17.2 us)
Async XLA Ops:
  0.0 13.6 %copy-start = (f32[1024,256]{1,0:T(8,128)S(1)}, f32[1024,256]{1,0:T(8,128)}, u32[]{:S(2)}) copy-start(f32[1024,256]{1,0:T(8,128)} %param.8) | copy-start | bytes 3145732
  2.1 31.9 %collective-permute-start.4 = (f32[64,2,8,128]{3,2,0,1:T(8,128)}, f32[64,2,8,128]{3,2,0,1:T(8,128)}, u32[]{:S(2)}, u32[]{:S(2)}) collective-permute-start(f32[64,2,8,128]{3,2,0,1:T(8,128)} %copy.20), channel_id=1, source_target_pairs={{0,248},{4,252},{8,0},{12,4},{16,8},{20,12},{24,16},{28,20},{32,24... | collective-permute-start | bytes 1572872 | tf_op jit(solution)/shard_map/ppermute | solution.py:12
  43.7 7.9 %copy-start.1 = (f32[1024,2,128]{2,0,1:T(8,128)S(1)}, f32[1024,2,128]{2,0,1:T(8,128)}, u32[]{:S(2)}) copy-start(f32[1024,2,128]{2,0,1:T(8,128)} %copy.30) | copy-start | bytes 3145732
  51.6 19.2 %collective-permute-start = (f32[64,2,8,128]{3,0,2,1:T(8,128)}, f32[64,2,8,128]{3,0,2,1:T(8,128)S(1)}, u32[]{:S(2)}, u32[]{:S(2)}) collective-permute-start(f32[64,2,8,128]{3,0,2,1:T(8,128)} %get-tuple-element.445), channel_id=1, source_target_pairs={{0,4},{4,8},{8,12},{12,16},{16,20},{20,24},{24,28},{28,32},{32,36}... | collective-permute-start | bytes 1572872 | tf_op jit(solution)/shard_map/while/body/eval_jaxpr/ppermute | solution.py:12
  51.6 22.9 %collective-permute-start.1 = (f32[2,8,64]{2,1,0:T(8,128)S(1)}, f32[2,8,64]{2,1,0:T(8,128)S(1)}, u32[]{:S(2)}, u32[]{:S(2)}) collective-permute-start(f32[2,8,64]{2,1,0:T(8,128)S(1)} %get-tuple-element.446), channel_id=1, source_target_pairs={{0,4},{4,8},{8,12},{12,16},{16,20},{20,24},{24,28},{28,32},{32,36}... | collective-permute-start | bytes 12296 | tf_op jit(solution)/shard_map/while/body/eval_jaxpr/ppermute | solution.py:12
  51.6 24.7 %collective-permute-start.2 = (f32[2,8,64]{2,1,0:T(8,128)S(1)}, f32[2,8,64]{2,1,0:T(8,128)S(1)}, u32[]{:S(2)}, u32[]{:S(2)}) collective-permute-start(f32[2,8,64]{2,1,0:T(8,128)S(1)} %get-tuple-element.447), channel_id=1, source_target_pairs={{0,4},{4,8},{8,12},{12,16},{16,20},{20,24},{24,28},{28,32},{32,36}... | collective-permute-start | bytes 12296 | tf_op jit(solution)/shard_map/while/body/eval_jaxpr/ppermute | solution.py:12
  51.7 29.3 %collective-permute-start.3 = (f32[64,2,8,128]{3,0,2,1:T(8,128)S(1)}, f32[64,2,8,128]{3,0,2,1:T(8,128)}, u32[]{:S(2)}, u32[]{:S(2)}) collective-permute-start(f32[64,2,8,128]{3,0,2,1:T(8,128)S(1)} %get-tuple-element.448), channel_id=1, source_target_pairs={{0,4},{4,8},{8,12},{12,16},{16,20},{20,24},{24,28},{28,32},{32,36}... | collective-permute-start | bytes 1572872 | tf_op jit(solution)/shard_map/while/body/eval_jaxpr/ppermute | solution.py:12
  86.4 19.3 %collective-permute-start = (f32[64,2,8,128]{3,0,2,1:T(8,128)}, f32[64,2,8,128]{3,0,2,1:T(8,128)S(1)}, u32[]{:S(2)}, u32[]{:S(2)}) collective-permute-start(f32[64,2,8,128]{3,0,2,1:T(8,128)} %get-tuple-element.445), channel_id=1, source_target_pairs={{0,4},{4,8},{8,12},{12,16},{16,20},{20,24},{24,28},{28,32},{32,36}... | collective-permute-start | bytes 1572872 | tf_op jit(solution)/shard_map/while/body/eval_jaxpr/ppermute | solution.py:12
  86.5 22.9 %collective-permute-start.1 = (f32[2,8,64]{2,1,0:T(8,128)S(1)}, f32[2,8,64]{2,1,0:T(8,128)S(1)}, u32[]{:S(2)}, u32[]{:S(2)}) collective-permute-start(f32[2,8,64]{2,1,0:T(8,128)S(1)} %get-tuple-element.446), channel_id=1, source_target_pairs={{0,4},{4,8},{8,12},{12,16},{16,20},{20,24},{24,28},{28,32},{32,36}... | collective-permute-start | bytes 12296 | tf_op jit(solution)/shard_map/while/body/eval_jaxpr/ppermute | solution.py:12
  86.6 24.6 %collective-permute-start.2 = (f32[2,8,64]{2,1,0:T(8,128)S(1)}, f32[2,8,64]{2,1,0:T(8,128)S(1)}, u32[]{:S(2)}, u32[]{:S(2)}) collective-permute-start(f32[2,8,64]{2,1,0:T(8,128)S(1)} %get-tuple-element.447), channel_id=1, source_target_pairs={{0,4},{4,8},{8,12},{12,16},{16,20},{20,24},{24,28},{28,32},{32,36}... | collective-permute-start | bytes 12296 | tf_op jit(solution)/shard_map/while/body/eval_jaxpr/ppermute | solution.py:12
  86.7 28.4 %collective-permute-start.3 = (f32[64,2,8,128]{3,0,2,1:T(8,128)S(1)}, f32[64,2,8,128]{3,0,2,1:T(8,128)}, u32[]{:S(2)}, u32[]{:S(2)}) collective-permute-start(f32[64,2,8,128]{3,0,2,1:T(8,128)S(1)} %get-tuple-element.448), channel_id=1, source_target_pairs={{0,4},{4,8},{8,12},{12,16},{16,20},{20,24},{24,28},{28,32},{32,36}... | collective-permute-start | bytes 1572872 | tf_op jit(solution)/shard_map/while/body/eval_jaxpr/ppermute | solution.py:12
  120.5 19.3 %collective-permute-start = (f32[64,2,8,128]{3,0,2,1:T(8,128)}, f32[64,2,8,128]{3,0,2,1:T(8,128)S(1)}, u32[]{:S(2)}, u32[]{:S(2)}) collective-permute-start(f32[64,2,8,128]{3,0,2,1:T(8,128)} %get-tuple-element.445), channel_id=1, source_target_pairs={{0,4},{4,8},{8,12},{12,16},{16,20},{20,24},{24,28},{28,32},{32,36}... | collective-permute-start | bytes 1572872 | tf_op jit(solution)/shard_map/while/body/eval_jaxpr/ppermute | solution.py:12
  120.6 22.9 %collective-permute-start.1 = (f32[2,8,64]{2,1,0:T(8,128)S(1)}, f32[2,8,64]{2,1,0:T(8,128)S(1)}, u32[]{:S(2)}, u32[]{:S(2)}) collective-permute-start(f32[2,8,64]{2,1,0:T(8,128)S(1)} %get-tuple-element.446), channel_id=1, source_target_pairs={{0,4},{4,8},{8,12},{12,16},{16,20},{20,24},{24,28},{28,32},{32,36}... | collective-permute-start | bytes 12296 | tf_op jit(solution)/shard_map/while/body/eval_jaxpr/ppermute | solution.py:12
  120.7 24.6 %collective-permute-start.2 = (f32[2,8,64]{2,1,0:T(8,128)S(1)}, f32[2,8,64]{2,1,0:T(8,128)S(1)}, u32[]{:S(2)}, u32[]{:S(2)}) collective-permute-start(f32[2,8,64]{2,1,0:T(8,128)S(1)} %get-tuple-element.447), channel_id=1, source_target_pairs={{0,4},{4,8},{8,12},{12,16},{16,20},{20,24},{24,28},{28,32},{32,36}... | collective-permute-start | bytes 12296 | tf_op jit(solution)/shard_map/while/body/eval_jaxpr/ppermute | solution.py:12
  120.8 27.5 %collective-permute-start.3 = (f32[64,2,8,128]{3,0,2,1:T(8,128)S(1)}, f32[64,2,8,128]{3,0,2,1:T(8,128)}, u32[]{:S(2)}, u32[]{:S(2)}) collective-permute-start(f32[64,2,8,128]{3,0,2,1:T(8,128)S(1)} %get-tuple-element.448), channel_id=1, source_target_pairs={{0,4},{4,8},{8,12},{12,16},{16,20},{20,24},{24,28},{28,32},{32,36}... | collective-permute-start | bytes 1572872 | tf_op jit(solution)/shard_map/while/body/eval_jaxpr/ppermute | solution.py:12
  153.8 19.3 %collective-permute-start = (f32[64,2,8,128]{3,0,2,1:T(8,128)}, f32[64,2,8,128]{3,0,2,1:T(8,128)S(1)}, u32[]{:S(2)}, u32[]{:S(2)}) collective-permute-start(f32[64,2,8,128]{3,0,2,1:T(8,128)} %get-tuple-element.445), channel_id=1, source_target_pairs={{0,4},{4,8},{8,12},{12,16},{16,20},{20,24},{24,28},{28,32},{32,36}... | collective-permute-start | bytes 1572872 | tf_op jit(solution)/shard_map/while/body/eval_jaxpr/ppermute | solution.py:12
  153.9 22.9 %collective-permute-start.1 = (f32[2,8,64]{2,1,0:T(8,128)S(1)}, f32[2,8,64]{2,1,0:T(8,128)S(1)}, u32[]{:S(2)}, u32[]{:S(2)}) collective-permute-start(f32[2,8,64]{2,1,0:T(8,128)S(1)} %get-tuple-element.446), channel_id=1, source_target_pairs={{0,4},{4,8},{8,12},{12,16},{16,20},{20,24},{24,28},{28,32},{32,36}... | collective-permute-start | bytes 12296 | tf_op jit(solution)/shard_map/while/body/eval_jaxpr/ppermute | solution.py:12
  153.9 24.6 %collective-permute-start.2 = (f32[2,8,64]{2,1,0:T(8,128)S(1)}, f32[2,8,64]{2,1,0:T(8,128)S(1)}, u32[]{:S(2)}, u32[]{:S(2)}) collective-permute-start(f32[2,8,64]{2,1,0:T(8,128)S(1)} %get-tuple-element.447), channel_id=1, source_target_pairs={{0,4},{4,8},{8,12},{12,16},{16,20},{20,24},{24,28},{28,32},{32,36}... | collective-permute-start | bytes 12296 | tf_op jit(solution)/shard_map/while/body/eval_jaxpr/ppermute | solution.py:12
  154.0 26.7 %collective-permute-start.3 = (f32[64,2,8,128]{3,0,2,1:T(8,128)S(1)}, f32[64,2,8,128]{3,0,2,1:T(8,128)}, u32[]{:S(2)}, u32[]{:S(2)}) collective-permute-start(f32[64,2,8,128]{3,0,2,1:T(8,128)S(1)} %get-tuple-element.448), channel_id=1, source_target_pairs={{0,4},{4,8},{8,12},{12,16},{16,20},{20,24},{24,28},{28,32},{32,36}... | collective-permute-start | bytes 1572872 | tf_op jit(solution)/shard_map/while/body/eval_jaxpr/ppermute | solution.py:12
  186.1 19.3 %collective-permute-start = (f32[64,2,8,128]{3,0,2,1:T(8,128)}, f32[64,2,8,128]{3,0,2,1:T(8,128)S(1)}, u32[]{:S(2)}, u32[]{:S(2)}) collective-permute-start(f32[64,2,8,128]{3,0,2,1:T(8,128)} %get-tuple-element.445), channel_id=1, source_target_pairs={{0,4},{4,8},{8,12},{12,16},{16,20},{20,24},{24,28},{28,32},{32,36}... | collective-permute-start | bytes 1572872 | tf_op jit(solution)/shard_map/while/body/eval_jaxpr/ppermute | solution.py:12
  186.2 22.9 %collective-permute-start.1 = (f32[2,8,64]{2,1,0:T(8,128)S(1)}, f32[2,8,64]{2,1,0:T(8,128)S(1)}, u32[]{:S(2)}, u32[]{:S(2)}) collective-permute-start(f32[2,8,64]{2,1,0:T(8,128)S(1)} %get-tuple-element.446), channel_id=1, source_target_pairs={{0,4},{4,8},{8,12},{12,16},{16,20},{20,24},{24,28},{28,32},{32,36}... | collective-permute-start | bytes 12296 | tf_op jit(solution)/shard_map/while/body/eval_jaxpr/ppermute | solution.py:12
  186.3 24.6 %collective-permute-start.2 = (f32[2,8,64]{2,1,0:T(8,128)S(1)}, f32[2,8,64]{2,1,0:T(8,128)S(1)}, u32[]{:S(2)}, u32[]{:S(2)}) collective-permute-start(f32[2,8,64]{2,1,0:T(8,128)S(1)} %get-tuple-element.447), channel_id=1, source_target_pairs={{0,4},{4,8},{8,12},{12,16},{16,20},{20,24},{24,28},{28,32},{32,36}... | collective-permute-start | bytes 12296 | tf_op jit(solution)/shard_map/while/body/eval_jaxpr/ppermute | solution.py:12
  186.4 25.8 %collective-permute-start.3 = (f32[64,2,8,128]{3,0,2,1:T(8,128)S(1)}, f32[64,2,8,128]{3,0,2,1:T(8,128)}, u32[]{:S(2)}, u32[]{:S(2)}) collective-permute-start(f32[64,2,8,128]{3,0,2,1:T(8,128)S(1)} %get-tuple-element.448), channel_id=1, source_target_pairs={{0,4},{4,8},{8,12},{12,16},{16,20},{20,24},{24,28},{28,32},{32,36}... | collective-permute-start | bytes 1572872 | tf_op jit(solution)/shard_map/while/body/eval_jaxpr/ppermute | solution.py:12
  217.7 33.0 %collective-permute-start.5 = (f32[64,2,8,128]{3,0,2,1:T(8,128)S(1)}, f32[64,2,8,128]{3,0,2,1:T(8,128)S(1)}, u32[]{:S(2)}, u32[]{:S(2)}) collective-permute-start(f32[64,2,8,128]{3,0,2,1:T(8,128)S(1)} %get-tuple-element.292), channel_id=1, source_target_pairs={{0,244},{4,248},{8,252},{12,0},{16,4},{20,8},{24,12},{28,16},{32,2... | collective-permute-start | bytes 1572872 | tf_op jit(solution)/shard_map/ppermute | solution.py:12
  217.8 32.9 %collective-permute-start.6 = (f32[2,8,64]{2,1,0:T(8,128)S(1)}, f32[2,8,64]{2,1,0:T(8,128)S(1)}, u32[]{:S(2)}, u32[]{:S(2)}) collective-permute-start(f32[2,8,64]{2,1,0:T(8,128)S(1)} %get-tuple-element.293), channel_id=1, source_target_pairs={{0,244},{4,248},{8,252},{12,0},{16,4},{20,8},{24,12},{28,16},{32,2... | collective-permute-start | bytes 12296 | tf_op jit(solution)/shard_map/ppermute | solution.py:12
where the time goes:
time: 253 us; the launch traced here: 252 us
  waiting for transfers between devices  155 us (61%)
  matrix products  57.5 us (23%)
  starting transfers between devices  13.7 us (5%)
  other arithmetic  12.9 us (5%)
  local copies, waits for them, and re-layouts  11.9 us (5%)
    ppermute x23, waiting for transfers between devices, passed_along(): lax.ppermute(shard, axis, [(i, (i + by) % size) for i in range(size)])  155 us
    dot_general x6, matrix products, attend(): jnp.einsum('hgqk,khd->qhgd', weights, value_tile, precision=lax.Precision...  32.9 us
    dot_general x6, matrix products, attend(): jnp.einsum('qhgd,khd->hgqk', query_tile, key_tile, precision=lax.Precisio...  24.5 us
    ppermute x23, starting transfers between devices, passed_along(): lax.ppermute(shard, axis, [(i, (i + by) % size) for i in range(size)])  13.7 us
    reduce_sum x6, other arithmetic, attend(): weight_sum = weight_sum * factor + jnp.sum(weights, axis=-1)  8.12 us
    unnamed x14, local copies, waits for them, and re-layouts  6.76 us
  transfers between devices with their start and end apart: 23, of which 12 were waited for; matrix products, arithmetic and copies ran while one was open for 14% of the time, Pallas kernels for 0%

commit v1 on v0

v1 whole, which is shorter than its diff:
```python
import functools
import jax
import jax.numpy as jnp
from jax import lax
from jax.experimental import pallas as pl
from jax.experimental.pallas import tpu as pltpu
from jax.sharding import PartitionSpec as P

HEAD_DIM = 128
LOG2E = 1.4426950408889634
LOW = -1e30
CHUNK = 256
LANES = 128
GROUP = 8


def split(x):
    high = x.astype(jnp.bfloat16)
    return high, (x - high.astype(jnp.float32)).astype(jnp.bfloat16)


def query_side(q_ref, h):
    parts = []
    for g in range(h * GROUP, (h + 1) * GROUP):
        high, low = split(q_ref[:, g * HEAD_DIM:(g + 1) * HEAD_DIM] * (HEAD_DIM ** -0.5 * LOG2E))
        parts.append(jnp.concatenate([high, low, high, low], axis=1))
    return jnp.concatenate(parts, axis=0)


def attend(count, q_side, key_chunk, value_chunk, blocks, scores_ref, store):
    width = q_side.shape[0]
    top = jnp.full((8, width), LOW, jnp.float32)
    for c in range(blocks):
        high, low = key_chunk(c)
        k_side = jnp.concatenate([high, high, low, low], axis=1)
        s = lax.dot_general(k_side, q_side, (((1,), (1,)), ((), ())), preferred_element_type=jnp.float32)
        row = lax.broadcasted_iota(jnp.int32, (CHUNK, width), 0) + c * CHUNK
        s = jnp.where(row < count, s, LOW)
        scores_ref[c * CHUNK:(c + 1) * CHUNK, :] = s
        top = jnp.maximum(top, jnp.max(s.reshape(CHUNK // 8, 8, width), axis=0))
    peak = jnp.max(top, axis=0, keepdims=True)
    total = jnp.zeros((8, width), jnp.float32)
    acc = None
    for c in range(blocks):
        p = jnp.exp2(scores_ref[c * CHUNK:(c + 1) * CHUNK, :] - peak)
        total = total + jnp.sum(p.reshape(CHUNK // 8, 8, width), axis=0)
        p_high, p_low = split(p)
        sides = value_chunk(c)
        both = jnp.dot(sides, p_high, preferred_element_type=jnp.float32)
        term = both[:HEAD_DIM] + both[HEAD_DIM:] + jnp.dot(sides[:HEAD_DIM], p_low, preferred_element_type=jnp.float32)
        acc = term if acc is None else acc + term
    store(acc, peak, jnp.sum(total, axis=0, keepdims=True))


def store_part(out_ref, i, acc, peak, mass):
    tiles = acc.shape[1] // LANES
    base = tiles * HEAD_DIM
    for j in range(tiles):
        lanes = slice(j * LANES, (j + 1) * LANES)
        out_ref[i, j * HEAD_DIM:(j + 1) * HEAD_DIM, :] = acc[:, lanes]
        out_ref[i, base + j:base + j + 1, :] = peak[:, lanes]
        out_ref[i, base + tiles + j:base + tiles + j + 1, :] = mass[:, lanes]


def side_chunks(k_sides_ref, v_sides_ref, h):
    def keys(c):
        rows = slice(c * CHUNK, (c + 1) * CHUNK)
        return k_sides_ref[h, rows, :HEAD_DIM], k_sides_ref[h, rows, HEAD_DIM:]

    def values(c):
        return v_sides_ref[h, :, c * CHUNK:(c + 1) * CHUNK]

    return keys, values


def own_kernel(info_ref, q_ref, k_ref, v_ref, out_ref, k_sides_ref, v_sides_ref, scores_ref):
    blocks = k_ref.shape[0] // CHUNK
    for h in range(out_ref.shape[0]):
        cols = slice(h * HEAD_DIM, (h + 1) * HEAD_DIM)
        for c in range(blocks):
            rows = slice(c * CHUNK, (c + 1) * CHUNK)
            high, low = split(k_ref[rows, cols])
            k_sides_ref[h, rows, :HEAD_DIM] = high
            k_sides_ref[h, rows, HEAD_DIM:] = low
            high, low = split(v_ref[rows, cols].T)
            v_sides_ref[h, :HEAD_DIM, rows] = high
            v_sides_ref[h, HEAD_DIM:, rows] = low
        attend(info_ref[1], query_side(q_ref, h), *side_chunks(k_sides_ref, v_sides_ref, h), blocks, scores_ref,
               functools.partial(store_part, out_ref, h))


WHOLE = pl.BlockSpec(memory_space=pltpu.VMEM)


def own_visit(info, q, keys, values):
    rows = keys.shape[0]
    n = keys.shape[1] // HEAD_DIM
    width = q.shape[0] * GROUP
    tall = (width // LANES) * (HEAD_DIM + 2)
    return pl.pallas_call(
        own_kernel,
        in_specs=[pl.BlockSpec(memory_space=pltpu.SMEM), WHOLE, WHOLE, WHOLE],
        out_specs=(WHOLE, WHOLE, WHOLE),
        out_shape=(
            jax.ShapeDtypeStruct((n, tall, LANES), jnp.float32),
            jax.ShapeDtypeStruct((n, rows, 2 * HEAD_DIM), jnp.bfloat16),
            jax.ShapeDtypeStruct((n, 2 * HEAD_DIM, rows), jnp.bfloat16),
        ),
        scratch_shapes=[pltpu.VMEM((rows, width), jnp.float32)],
        cost_estimate=pl.CostEstimate(flops=n * 12 * width * rows * HEAD_DIM, bytes_accessed=n * 2**20 * 2, transcendentals=n * width * rows),
        compiler_params=pltpu.CompilerParams(vmem_limit_bytes=14 * 2**20),
    )(info, q, keys, values)


def visit_kernel(heads, q_heads, info_ref, q_ref, k_sides_ref, v_sides_ref, out_ref, scores_ref):
    usable = info_ref[0]
    tiles = scores_ref.shape[1] // LANES

    @pl.when(usable > 0)
    def _():
        for i, (h, q_h) in enumerate(zip(heads, q_heads)):
            attend(info_ref[1], query_side(q_ref, q_h), *side_chunks(k_sides_ref, v_sides_ref, h),
                   scores_ref.shape[0] // CHUNK, scores_ref, functools.partial(store_part, out_ref, i))

    @pl.when(usable <= 0)
    def _():
        which = lax.broadcasted_iota(jnp.int32, (2 * tiles, LANES), 0)
        for i in range(len(heads)):
            out_ref[i, :tiles * HEAD_DIM, :] = jnp.zeros((tiles * HEAD_DIM, LANES), jnp.float32)
            out_ref[i, tiles * HEAD_DIM:, :] = jnp.where(which < tiles, LOW, 0.0)


def visit(info, q, sides, heads, q_heads):
    k_sides, v_sides = sides
    n = len(heads)
    rows = k_sides.shape[1]
    width = q.shape[0] * GROUP
    tall = (width // LANES) * (HEAD_DIM + 2)
    return pl.pallas_call(
        functools.partial(visit_kernel, heads, q_heads),
        in_specs=[pl.BlockSpec(memory_space=pltpu.SMEM), WHOLE, WHOLE, WHOLE],
        out_specs=WHOLE,
        out_shape=jax.ShapeDtypeStruct((n, tall, LANES), jnp.float32),
        scratch_shapes=[pltpu.VMEM((rows, width), jnp.float32)],
        cost_estimate=pl.CostEstimate(flops=n * 12 * width * rows * HEAD_DIM, bytes_accessed=2**20 * 2, transcendentals=n * width * rows),
        compiler_params=pltpu.CompilerParams(vmem_limit_bytes=10 * 2**20),
    )(info, q, k_sides, v_sides)


def combined(parts, j, tiles):
    base = tiles * HEAD_DIM
    peaks = [r[i, base + j:base + j + 1, :] for r, i in parts]
    peak = functools.reduce(jnp.maximum, peaks)
    acc = 0.0
    mass = 0.0
    for (r, i), one in zip(parts, peaks):
        factor = jnp.exp2(one - peak)
        acc = acc + r[i, j * HEAD_DIM:(j + 1) * HEAD_DIM, :] * factor
        mass = mass + r[i, base + tiles + j:base + tiles + j + 1, :] * factor
    return peak, acc, mass


def merge_kernel(first, a_ref, b_ref, out_ref):
    n, tall, _ = out_ref.shape
    tiles = tall // (HEAD_DIM + 2)
    base = tiles * HEAD_DIM
    for i in range(n):
        for j in range(tiles):
            peak, acc, mass = combined(((a_ref, first + i), (b_ref, i)), j, tiles)
            out_ref[i, j * HEAD_DIM:(j + 1) * HEAD_DIM, :] = acc
            out_ref[i, base + j:base + j + 1, :] = peak
            out_ref[i, base + tiles + j:base + tiles + j + 1, :] = mass


def merge(a, b, first=0):
    n, tall, lanes = b.shape
    return pl.pallas_call(
        functools.partial(merge_kernel, first),
        in_specs=[WHOLE, WHOLE],
        out_specs=WHOLE,
        out_shape=jax.ShapeDtypeStruct(b.shape, jnp.float32),
        cost_estimate=pl.CostEstimate(flops=3 * n * tall * lanes, bytes_accessed=12 * n * tall * lanes, transcendentals=0),
        compiler_params=pltpu.CompilerParams(vmem_limit_bytes=4 * 2**20),
    )(a, b)


def finish_kernel(own_ref, left_ref, right_a_ref, right_b_ref, out_ref):
    tiles = own_ref.shape[1] // (HEAD_DIM + 2)
    tokens = out_ref.shape[0]
    per = LANES // tokens
    for i, right_ref in enumerate((right_a_ref, right_b_ref)):
        for j in range(tiles):
            _, acc, mass = combined(((own_ref, i), (left_ref, i), (right_ref, 0)), j, tiles)
            normed = (acc / mass).T
            for g in range(per):
                head = (i * tiles + j) * per + g
                out_ref[:, head * HEAD_DIM:(head + 1) * HEAD_DIM] = normed[g * tokens:(g + 1) * tokens, :]


def finish(own, left, right_a, right_b, shape):
    return pl.pallas_call(
        finish_kernel,
        in_specs=[WHOLE] * 4,
        out_specs=WHOLE,
        out_shape=jax.ShapeDtypeStruct(shape, jnp.float32),
        cost_estimate=pl.CostEstimate(flops=10 * own.size, bytes_accessed=16 * own.size, transcendentals=0),
        compiler_params=pltpu.CompilerParams(vmem_limit_bytes=8 * 2**20),
    )(own, left, right_a, right_b)


def shift(x, by):
    size = lax.axis_size("blk")
    return lax.ppermute(x, "blk", [(i, (i + by) % size) for i in range(size)])


def per_device(queries, visual_keys, projected_values, valid_lengths):
    size = lax.axis_size("blk")
    here = lax.axis_index("blk")
    half = queries.shape[1] // 2

    def info(offset):
        query_block = here - offset
        fits = (query_block >= 0) & (query_block < size)
        return jnp.stack([fits.astype(jnp.int32), valid_lengths[0]])

    def look(q, offset, heads=(0, 1), q_heads=(0, 1)):
        return visit(info(offset), q, sides, heads, q_heads)

    f1 = shift(queries, 1)
    g1 = shift(queries, -1)
    own, *sides = own_visit(info(0), queries, visual_keys, projected_values)
    f2 = shift(f1, 1)
    g2 = shift(g1, -1)
    cf1 = look(f1, 1)
    cg1 = look(g1, -1)
    f3a = shift(f2[:, :half], 1)
    f3b = shift(f2[:, half:], 1)
    cg2 = look(g2, -2)
    r2 = shift(cg2, 1)
    cf2a = look(f2, 2, (0,), (0,))
    cf3a = look(f3a, 3, (0,), (0,))
    s3a = shift(cf3a, -1)
    cf2b = look(f2, 2, (1,), (1,))
    cf3b = look(f3b, 3, (1,), (0,))
    s3b = shift(cf3b, -1)
    s2a = shift(merge(cf2a, s3a), -1)
    r1 = shift(merge(cg1, r2), 1)
    s2b = shift(merge(cf2b, s3b), -1)
    s1a = shift(merge(cf1, s2a, 0), -1)
    s1b = shift(merge(cf1, s2b, 1), -1)
    return finish(own, r1, s1a, s1b, queries.shape)


def solution(mesh):
    return jax.shard_map(
        per_device,
        mesh=mesh,
        in_specs=(P("blk", "heads"), P("blk", "heads"), P("blk", "heads"), P("blk")),
        out_specs=P("blk", "heads"),
        check_vma=False,
    )
```

time: 253 us -> 93.5 us (0.37)
  waiting for transfers between devices: 155 us -> 34.7 us
  matrix products: 57.5 us -> 0 us
  starting transfers between devices: 13.7 us -> 35.8 us
  Pallas kernels: 0 us -> 15.4 us
  other arithmetic: 12.9 us -> 0.45 us
  local copies, waits for them, and re-layouts: 11.9 us -> 5.99 us
    ppermute x23 -> x14, waiting for transfers between devices: 155 us -> 34.7 us  [shift(): return lax.ppermute(x, 'blk', [(i, (i + by) % size) for i in range(size)])]
    dot_general x12 -> x0, matrix products: 57.5 us -> none  [the longest x6 32.9 us: attend(): jnp.einsum('hgqk,khd->qhgd', weights, value_tile, precision=lax.Precision...]
    ppermute x23 -> x14, starting transfers between devices: 13.7 us -> 35.8 us  [shift(): return lax.ppermute(x, 'blk', [(i, (i + by) % size) for i in range(size)])]
    pallas_call x0 -> x14, Pallas kernels: none -> 15.4 us  [the longest x7 10.4 us: visit(): pl.pallas_call(functools.partial(visit_kernel, heads, q_heads), in_specs=...]
    reduce_sum x6 -> x0, other arithmetic: 8.12 us -> none  [attend(): weight_sum = weight_sum * factor + jnp.sum(weights, axis=-1)]
    while x5 -> x0, local copies, waits for them, and re-layouts: 4 us -> none
    and x6 -> x0, other arithmetic: 3.28 us -> none  [query_usable(): return own_usable & (owner_block >= 0) & (owner_block < shard_blocks)]
  transfers between devices with their start and end apart: 23 -> 14, of which waited for: 12 -> 6; matrix products, arithmetic and copies ran while one was open for 14% -> 1% of each run, Pallas kernels for 0% -> 15%
where the time goes in v1:
time: 93.5 us; the launch traced here: 93.2 us
  starting transfers between devices  35.8 us (38%)
  waiting for transfers between devices  34.7 us (37%)
  Pallas kernels  15.4 us (16%)
  local copies, waits for them, and re-layouts  5.99 us (6%)
    ppermute x14, starting transfers between devices, shift(): return lax.ppermute(x, 'blk', [(i, (i + by) % size) for i in range(size)])  35.8 us
    ppermute x14, waiting for transfers between devices, shift(): return lax.ppermute(x, 'blk', [(i, (i + by) % size) for i in range(size)])  34.7 us
    pallas_call x7, Pallas kernels, visit(): pl.pallas_call(functools.partial(visit_kernel, heads, q_heads), in_specs=...  10.4 us
    unnamed x14, local copies, waits for them, and re-layouts  5.95 us
    pallas_call x1, Pallas kernels, own_visit(): pl.pallas_call(own_kernel, in_specs=[pl.BlockSpec(memory_space=pltpu.SMEM...  3.72 us
  transfers between devices with their start and end apart: 14, of which 6 were waited for; matrix products, arithmetic and copies ran while one was open for 1% of the time, Pallas kernels for 15%

profile of v1, /device:TPU:16, one launch (start us, length us, event | category | flops | bytes accessed | tf_op | source)
XLA Modules:
  0.0 93.2 jit_solution(3625958459983536206)
XLA Ops:
  0.0 1.9 %collective-permute-start.4 = (f32[64,2048]{1,0:T(8,128)}, f32[64,2048]{1,0:T(8,128)S(1)}, u32[]{:S(2)}, u32[]{:S(2)}) collective-permute-start(f32[64,2048]{1,0:T(8,128)} %q_ref.1), channel_id=1, source_target_pairs={{0,4},{4,8},{8,12},{12,16},{16,20},{20,24},{24,28},{28,32},{32,36}... | collective-permute-start | bytes 1572872 | tf_op jit(solution)/shard_map/ppermute | solution.py:213
  1.9 6.9 %collective-permute-start = (f32[64,2048]{1,0:T(8,128)}, f32[64,2048]{1,0:T(8,128)S(1)}, u32[]{:S(2)}, u32[]{:S(2)}) collective-permute-start(f32[64,2048]{1,0:T(8,128)} %q_ref.1), channel_id=1, source_target_pairs={{0,252},{4,0},{8,4},{12,8},{16,12},{20,16},{24,20},{28,24},{32,28}... | collective-permute-start | bytes 1572872 | tf_op jit(solution)/shard_map/ppermute | solution.py:213
  9.4 11.5 %collective-permute-done.4.q_ref = f32[64,2048]{1,0:T(8,128)S(1)} collective-permute-done((f32[64,2048]{1,0:T(8,128)}, f32[64,2048]{1,0:T(8,128)S(1)}, u32[]{:S(2)}, u32[]{:S(2)}) %collective-permute-start.4) | collective-permute-done | bytes 524320 | tf_op jit(solution)/shard_map/ppermute | solution.py:213
  21.1 6.3 %collective-permute-start.1 = (f32[64,2048]{1,0:T(8,128)S(1)}, f32[64,2048]{1,0:T(8,128)S(1)}, u32[]{:S(2)}, u32[]{:S(2)}) collective-permute-start(f32[64,2048]{1,0:T(8,128)S(1)} %collective-permute-done.q_ref), channel_id=1, source_target_pairs={{0,252},{4,0},{8,4},{12,8},{16,12},{20,16},{24,20},{28,24},{32,28}... | collective-permute-start | bytes 1572872 | tf_op jit(solution)/shard_map/ppermute | solution.py:213
  27.5 1.2 %copy-done = f32[1024,256]{1,0:T(8,128)S(1)} copy-done((f32[1024,256]{1,0:T(8,128)S(1)}, f32[1024,256]{1,0:T(8,128)}, u32[]{:S(2)}) %copy-start) | copy-done | bytes 1048600
  28.7 1.2 %copy-done.1 = f32[1024,256]{1,0:T(8,128)S(1)} copy-done((f32[1024,256]{1,0:T(8,128)S(1)}, f32[1024,256]{1,0:T(8,128)}, u32[]{:S(2)}) %copy-start.1) | copy-done | bytes 1048600
  29.9 1.0 %copy-done.2 = f32[64,2048]{1,0:T(8,128)S(1)} copy-done((f32[64,2048]{1,0:T(8,128)S(1)}, f32[64,2048]{1,0:T(8,128)}, u32[]{:S(2)}) %copy-start.2) | copy-done | bytes 524312
  31.0 3.7 %shard_map.46 = (f32[2,520,128]{2,1,0:T(8,128)S(1)}, bf16[2,1024,256]{2,1,0:T(8,128)(2,1)S(1)}, bf16[2,256,1024]{2,1,0:T(8,128)(2,1)S(1)}) custom-call(s32[2]{0:T(128)S(1)} %pad_add_fusion.info_ref, f32[64,2048]{1,0:T(8,128)S(1)} %copy-done.2, f32[1024,256]{1,0:T(8,128)S(1)} %copy-done, f32[1024,256]{1,0:T(8,128)S(1)} %copy-done.1), custom_call_target="tpu_custom_call" | custom-call | flops 1610612736 | bytes 4194304 | tf_op jit(solution)/shard_map/pallas_call | solution.py:100
  34.7 3.5 %collective-permute-done.5.q_ref = f32[64,2048]{1,0:T(8,128)S(1)} collective-permute-done((f32[64,2048]{1,0:T(8,128)S(1)}, f32[64,2048]{1,0:T(8,128)S(1)}, u32[]{:S(2)}, u32[]{:S(2)}) %collective-permute-start.5) | collective-permute-done | bytes 524320 | tf_op jit(solution)/shard_map/ppermute | solution.py:213
  38.3 0.1 collective-permute-start.10
  38.5 3.7 %shard_map.48 = f32[2,520,128]{2,1,0:T(8,128)S(1)} custom-call(s32[2]{0:T(128)S(1)} %pad_add_fusion.2.info_ref, f32[64,2048]{1,0:T(8,128)S(1)} %collective-permute-done.1.q_ref, bf16[2,1024,256]{2,1,0:T(8,128)(2,1)S(1)} %get-tuple-element.9.k_sides_ref, bf16[2,256,1024]{2,1,0:T(8,128)(2,1)S(1)} %get-tuple-element.10.v_sides_ref), custom_call_target="tpu_custom_call" | custom-call | flops 1610612736 | bytes 2097152 | tf_op jit(solution)/shard_map/pallas_call | solution.py:139
  42.3 9.4 %collective-permute-done.10.q_ref = f32[64,1024]{1,0:T(8,128)S(1)} collective-permute-done((f32[64,1024]{1,0:T(8,128)S(1)}, f32[64,1024]{1,0:T(8,128)S(1)}, u32[]{:S(2)}, u32[]{:S(2)}) %collective-permute-start.10) | collective-permute-done | bytes 262176 | tf_op jit(solution)/shard_map/ppermute | solution.py:213
  51.7 0.7 shard_map.56
  52.5 1.2 %collective-permute-start.11 = (f32[1,520,128]{2,1,0:T(8,128)S(1)}, f32[1,520,128]{2,1,0:T(8,128)S(1)}, u32[]{:S(2)}, u32[]{:S(2)}) collective-permute-start(f32[1,520,128]{2,1,0:T(8,128)S(1)} %shard_map.56), channel_id=1, source_target_pairs={{0,252},{4,0},{8,4},{12,8},{16,12},{20,16},{24,20},{28,24},{32,28}... | collective-permute-start | bytes 798728 | tf_op jit(solution)/shard_map/ppermute | solution.py:213
  53.7 3.6 %collective-permute-done.6.q_ref = f32[64,1024]{1,0:T(8,128)S(1)} collective-permute-done((f32[64,1024]{1,0:T(8,128)S(1)}, f32[64,1024]{1,0:T(8,128)S(1)}, u32[]{:S(2)}, u32[]{:S(2)}) %collective-permute-start.6) | collective-permute-done | bytes 262176 | tf_op jit(solution)/shard_map/ppermute | solution.py:213
  57.3 0.6 shard_map.52
  57.9 1.2 %collective-permute-start.7 = (f32[1,520,128]{2,1,0:T(8,128)S(1)}, f32[1,520,128]{2,1,0:T(8,128)S(1)}, u32[]{:S(2)}, u32[]{:S(2)}) collective-permute-start(f32[1,520,128]{2,1,0:T(8,128)S(1)} %shard_map.52), channel_id=1, source_target_pairs={{0,252},{4,0},{8,4},{12,8},{16,12},{20,16},{24,20},{28,24},{32,28}... | collective-permute-start | bytes 798728 | tf_op jit(solution)/shard_map/ppermute | solution.py:213
  59.2 3.7 %shard_map.47.a_ref = f32[2,520,128]{2,1,0:T(8,128)S(1)} custom-call(s32[2]{0:T(128)S(1)} %pad_add_fusion.1.info_ref, f32[64,2048]{1,0:T(8,128)S(1)} %collective-permute-done.q_ref, bf16[2,1024,256]{2,1,0:T(8,128)(2,1)S(1)} %get-tuple-element.9.k_sides_ref, bf16[2,256,1024]{2,1,0:T(8,128)(2,1)S(1)} %get-tuple-element.10.v_sides_ref), custom_call_target="tpu_custom_call" | custom-call | flops 1610612736 | bytes 2097152 | tf_op jit(solution)/shard_map/pallas_call | solution.py:139
  62.8 0.6 shard_map.55.a_ref
  63.4 0.6 shard_map.51.a_ref
  64.1 3.3 %collective-permute-start.12 = (f32[1,520,128]{2,1,0:T(8,128)S(1)}, f32[1,520,128]{2,1,0:T(8,128)S(1)}, u32[]{:S(2)}, u32[]{:S(2)}) collective-permute-start(f32[1,520,128]{2,1,0:T(8,128)S(1)} %shard_map.57), channel_id=1, source_target_pairs={{0,252},{4,0},{8,4},{12,8},{16,12},{20,16},{24,20},{28,24},{32,28}... | collective-permute-start | bytes 798728 | tf_op jit(solution)/shard_map/ppermute | solution.py:213
  67.4 5.1 %collective-permute-start.8 = (f32[1,520,128]{2,1,0:T(8,128)S(1)}, f32[1,520,128]{2,1,0:T(8,128)S(1)}, u32[]{:S(2)}, u32[]{:S(2)}) collective-permute-start(f32[1,520,128]{2,1,0:T(8,128)S(1)} %shard_map.53), channel_id=1, source_target_pairs={{0,252},{4,0},{8,4},{12,8},{16,12},{20,16},{24,20},{28,24},{32,28}... | collective-permute-start | bytes 798728 | tf_op jit(solution)/shard_map/ppermute | solution.py:213
  72.5 0.1 shard_map.49
  72.6 0.3 collective-permute-start.3
  73.0 1.2 %copy-done.4 = bf16[2,1024,256]{2,1,0:T(8,128)(2,1)S(1)} copy-done((bf16[2,1024,256]{2,1,0:T(8,128)(2,1)S(1)}, bf16[2,1024,256]{2,1,0:T(8,128)(2,1)}, u32[]{:S(2)}) %copy-start.4) | copy-done | bytes 1048600
  74.2 1.2 %copy-done.6 = bf16[2,256,1024]{2,1,0:T(8,128)(2,1)S(1)} copy-done((bf16[2,256,1024]{2,1,0:T(8,128)(2,1)S(1)}, bf16[2,256,1024]{2,1,0:T(8,128)(2,1)}, u32[]{:S(2)}) %copy-start.6) | copy-done | bytes 1048600
  75.4 0.6 shard_map.50.a_ref
  76.1 9.3 %collective-permute-start.13 = (f32[1,520,128]{2,1,0:T(8,128)S(1)}, f32[1,520,128]{2,1,0:T(8,128)S(1)}, u32[]{:S(2)}, u32[]{:S(2)}) collective-permute-start(f32[1,520,128]{2,1,0:T(8,128)S(1)} %shard_map.58), channel_id=1, source_target_pairs={{0,252},{4,0},{8,4},{12,8},{16,12},{20,16},{24,20},{28,24},{32,28}... | collective-permute-start | bytes 798728 | tf_op jit(solution)/shard_map/ppermute | solution.py:213
  85.5 0.1 collective-permute-start.9
  85.6 3.8 %collective-permute-done.13.right_b_ref = f32[1,520,128]{2,1,0:T(8,128)S(1)} collective-permute-done((f32[1,520,128]{2,1,0:T(8,128)S(1)}, f32[1,520,128]{2,1,0:T(8,128)S(1)}, u32[]{:S(2)}, u32[]{:S(2)}) %collective-permute-start.13) | collective-permute-done | bytes 266272 | tf_op jit(solution)/shard_map/ppermute | solution.py:213
  89.3 2.9 %collective-permute-done.9.right_a_ref = f32[1,520,128]{2,1,0:T(8,128)S(1)} collective-permute-done((f32[1,520,128]{2,1,0:T(8,128)S(1)}, f32[1,520,128]{2,1,0:T(8,128)S(1)}, u32[]{:S(2)}, u32[]{:S(2)}) %collective-permute-start.9) | collective-permute-done | bytes 266272 | tf_op jit(solution)/shard_map/ppermute | solution.py:213
  92.2 1.0 %shard_map.59 = f32[64,2048]{1,0:T(8,128)} custom-call(f32[2,520,128]{2,1,0:T(8,128)S(1)} %get-tuple-element.8.own_ref, f32[2,520,128]{2,1,0:T(8,128)S(1)} %collective-permute-done.3.left_ref, f32[1,520,128]{2,1,0:T(8,128)S(1)} %collective-permute-done.9.right_a_ref, f32[1,520,128]{2,1,0:T(8,128)S(1)} %collective-permute-done.13.right_b_ref), custom_call_target="tpu_custom_call" | custom-call | flops 1331200 | bytes 2129920 | tf_op jit(solution)/shard_map/pallas_call | solution.py:201
  (31 shorter events, 0.9 us)
Async XLA Ops:
  0.0 20.9 %collective-permute-start.4 = (f32[64,2048]{1,0:T(8,128)}, f32[64,2048]{1,0:T(8,128)S(1)}, u32[]{:S(2)}, u32[]{:S(2)}) collective-permute-start(f32[64,2048]{1,0:T(8,128)} %q_ref.1), channel_id=1, source_target_pairs={{0,4},{4,8},{8,12},{12,16},{16,20},{20,24},{24,28},{28,32},{32,36}... | collective-permute-start | bytes 1572872 | tf_op jit(solution)/shard_map/ppermute | solution.py:213
  1.9 19.1 %collective-permute-start = (f32[64,2048]{1,0:T(8,128)}, f32[64,2048]{1,0:T(8,128)S(1)}, u32[]{:S(2)}, u32[]{:S(2)}) collective-permute-start(f32[64,2048]{1,0:T(8,128)} %q_ref.1), channel_id=1, source_target_pairs={{0,252},{4,0},{8,4},{12,8},{16,12},{20,16},{24,20},{28,24},{32,28}... | collective-permute-start | bytes 1572872 | tf_op jit(solution)/shard_map/ppermute | solution.py:213
  20.9 17.3 %collective-permute-start.5 = (f32[64,2048]{1,0:T(8,128)S(1)}, f32[64,2048]{1,0:T(8,128)S(1)}, u32[]{:S(2)}, u32[]{:S(2)}) collective-permute-start(f32[64,2048]{1,0:T(8,128)S(1)} %collective-permute-done.4.q_ref), channel_id=1, source_target_pairs={{0,4},{4,8},{8,12},{12,16},{16,20},{20,24},{24,28},{28,32},{32,36}... | collective-permute-start | bytes 1572872 | tf_op jit(solution)/shard_map/ppermute | solution.py:213
  21.1 17.4 %collective-permute-start.1 = (f32[64,2048]{1,0:T(8,128)S(1)}, f32[64,2048]{1,0:T(8,128)S(1)}, u32[]{:S(2)}, u32[]{:S(2)}) collective-permute-start(f32[64,2048]{1,0:T(8,128)S(1)} %collective-permute-done.q_ref), channel_id=1, source_target_pairs={{0,252},{4,0},{8,4},{12,8},{16,12},{20,16},{24,20},{28,24},{32,28}... | collective-permute-start | bytes 1572872 | tf_op jit(solution)/shard_map/ppermute | solution.py:213
  27.5 1.2 %copy-start = (f32[1024,256]{1,0:T(8,128)S(1)}, f32[1024,256]{1,0:T(8,128)}, u32[]{:S(2)}) copy-start(f32[1024,256]{1,0:T(8,128)} %k_ref.1) | copy-start | bytes 3145732
  28.7 1.2 %copy-start.1 = (f32[1024,256]{1,0:T(8,128)S(1)}, f32[1024,256]{1,0:T(8,128)}, u32[]{:S(2)}) copy-start(f32[1024,256]{1,0:T(8,128)} %v_ref.1) | copy-start | bytes 3145732
  29.9 1.0 %copy-start.2 = (f32[64,2048]{1,0:T(8,128)S(1)}, f32[64,2048]{1,0:T(8,128)}, u32[]{:S(2)}) copy-start(f32[64,2048]{1,0:T(8,128)} %q_ref.1) | copy-start | bytes 1572868
  34.7 28.7 %copy-start.3 = (bf16[2,1024,256]{2,1,0:T(8,128)(2,1)}, bf16[2,1024,256]{2,1,0:T(8,128)(2,1)S(1)}, u32[]{:S(2)}) copy-start(bf16[2,1024,256]{2,1,0:T(8,128)(2,1)S(1)} %get-tuple-element.9.k_sides_ref) | copy-start | bytes 3145732
  34.7 28.7 %copy-start.5 = (bf16[2,256,1024]{2,1,0:T(8,128)(2,1)}, bf16[2,256,1024]{2,1,0:T(8,128)(2,1)S(1)}, u32[]{:S(2)}) copy-start(bf16[2,256,1024]{2,1,0:T(8,128)(2,1)S(1)} %get-tuple-element.10.v_sides_ref) | copy-start | bytes 3145732
  38.3 13.5 %collective-permute-start.10 = (f32[64,1024]{1,0:T(8,128)S(1)}, f32[64,1024]{1,0:T(8,128)S(1)}, u32[]{:S(2)}, u32[]{:S(2)}) collective-permute-start(f32[64,1024]{1,0:T(8,128)S(1)} %get-tuple-element.11), channel_id=1, source_target_pairs={{0,4},{4,8},{8,12},{12,16},{16,20},{20,24},{24,28},{28,32},{32,36}... | collective-permute-start | bytes 786440 | tf_op jit(solution)/shard_map/ppermute | solution.py:213
  38.3 19.0 %collective-permute-start.6 = (f32[64,1024]{1,0:T(8,128)S(1)}, f32[64,1024]{1,0:T(8,128)S(1)}, u32[]{:S(2)}, u32[]{:S(2)}) collective-permute-start(f32[64,1024]{1,0:T(8,128)S(1)} %get-tuple-element.12), channel_id=1, source_target_pairs={{0,4},{4,8},{8,12},{12,16},{16,20},{20,24},{24,28},{28,32},{32,36}... | collective-permute-start | bytes 786440 | tf_op jit(solution)/shard_map/ppermute | solution.py:213
  42.1 30.4 %collective-permute-start.2 = (f32[2,520,128]{2,1,0:T(8,128)S(1)}, f32[2,520,128]{2,1,0:T(8,128)S(1)}, u32[]{:S(2)}, u32[]{:S(2)}) collective-permute-start(f32[2,520,128]{2,1,0:T(8,128)S(1)} %shard_map.48), channel_id=1, source_target_pairs={{0,4},{4,8},{8,12},{12,16},{16,20},{20,24},{24,28},{28,32},{32,36}... | collective-permute-start | bytes 1597448 | tf_op jit(solution)/shard_map/ppermute | solution.py:213
  52.5 11.5 %collective-permute-start.11 = (f32[1,520,128]{2,1,0:T(8,128)S(1)}, f32[1,520,128]{2,1,0:T(8,128)S(1)}, u32[]{:S(2)}, u32[]{:S(2)}) collective-permute-start(f32[1,520,128]{2,1,0:T(8,128)S(1)} %shard_map.56), channel_id=1, source_target_pairs={{0,252},{4,0},{8,4},{12,8},{16,12},{20,16},{24,20},{28,24},{32,28}... | collective-permute-start | bytes 798728 | tf_op jit(solution)/shard_map/ppermute | solution.py:213
  57.9 9.4 %collective-permute-start.7 = (f32[1,520,128]{2,1,0:T(8,128)S(1)}, f32[1,520,128]{2,1,0:T(8,128)S(1)}, u32[]{:S(2)}, u32[]{:S(2)}) collective-permute-start(f32[1,520,128]{2,1,0:T(8,128)S(1)} %shard_map.52), channel_id=1, source_target_pairs={{0,252},{4,0},{8,4},{12,8},{16,12},{20,16},{24,20},{28,24},{32,28}... | collective-permute-start | bytes 798728 | tf_op jit(solution)/shard_map/ppermute | solution.py:213
  64.1 12.0 %collective-permute-start.12 = (f32[1,520,128]{2,1,0:T(8,128)S(1)}, f32[1,520,128]{2,1,0:T(8,128)S(1)}, u32[]{:S(2)}, u32[]{:S(2)}) collective-permute-start(f32[1,520,128]{2,1,0:T(8,128)S(1)} %shard_map.57), channel_id=1, source_target_pairs={{0,252},{4,0},{8,4},{12,8},{16,12},{20,16},{24,20},{28,24},{32,28}... | collective-permute-start | bytes 798728 | tf_op jit(solution)/shard_map/ppermute | solution.py:213
  67.4 18.0 %collective-permute-start.8 = (f32[1,520,128]{2,1,0:T(8,128)S(1)}, f32[1,520,128]{2,1,0:T(8,128)S(1)}, u32[]{:S(2)}, u32[]{:S(2)}) collective-permute-start(f32[1,520,128]{2,1,0:T(8,128)S(1)} %shard_map.53), channel_id=1, source_target_pairs={{0,252},{4,0},{8,4},{12,8},{16,12},{20,16},{24,20},{28,24},{32,28}... | collective-permute-start | bytes 798728 | tf_op jit(solution)/shard_map/ppermute | solution.py:213
  72.6 19.6 %collective-permute-start.3 = (f32[2,520,128]{2,1,0:T(8,128)S(1)}, f32[2,520,128]{2,1,0:T(8,128)S(1)}, u32[]{:S(2)}, u32[]{:S(2)}) collective-permute-start(f32[2,520,128]{2,1,0:T(8,128)S(1)} %shard_map.49), channel_id=1, source_target_pairs={{0,4},{4,8},{8,12},{12,16},{16,20},{20,24},{24,28},{28,32},{32,36}... | collective-permute-start | bytes 1597448 | tf_op jit(solution)/shard_map/ppermute | solution.py:213
  73.0 1.2 %copy-start.4 = (bf16[2,1024,256]{2,1,0:T(8,128)(2,1)S(1)}, bf16[2,1024,256]{2,1,0:T(8,128)(2,1)}, u32[]{:S(2)}) copy-start(bf16[2,1024,256]{2,1,0:T(8,128)(2,1)} %copy-done.3) | copy-start | bytes 3145732
  74.2 1.2 %copy-start.6 = (bf16[2,256,1024]{2,1,0:T(8,128)(2,1)S(1)}, bf16[2,256,1024]{2,1,0:T(8,128)(2,1)}, u32[]{:S(2)}) copy-start(bf16[2,256,1024]{2,1,0:T(8,128)(2,1)} %copy-done.5) | copy-start | bytes 3145732
  76.1 13.3 %collective-permute-start.13 = (f32[1,520,128]{2,1,0:T(8,128)S(1)}, f32[1,520,128]{2,1,0:T(8,128)S(1)}, u32[]{:S(2)}, u32[]{:S(2)}) collective-permute-start(f32[1,520,128]{2,1,0:T(8,128)S(1)} %shard_map.58), channel_id=1, source_target_pairs={{0,252},{4,0},{8,4},{12,8},{16,12},{20,16},{24,20},{28,24},{32,28}... | collective-permute-start | bytes 798728 | tf_op jit(solution)/shard_map/ppermute | solution.py:213
  85.5 6.7 %collective-permute-start.9 = (f32[1,520,128]{2,1,0:T(8,128)S(1)}, f32[1,520,128]{2,1,0:T(8,128)S(1)}, u32[]{:S(2)}, u32[]{:S(2)}) collective-permute-start(f32[1,520,128]{2,1,0:T(8,128)S(1)} %shard_map.54), channel_id=1, source_target_pairs={{0,252},{4,0},{8,4},{12,8},{16,12},{20,16},{24,20},{28,24},{32,28}... | collective-permute-start | bytes 798728 | tf_op jit(solution)/shard_map/ppermute | solution.py:213
